TPU v7x, 512 devices: a whole 4x4x16 slice. The times are simulated.
512 devices in a mesh: pts: 16 (over x, z_hi, core), ctr: 32 (over z_lo, y).
Axes of the slice: x: 4, y: 4, z: 16 (z_hi: 2, z_lo: 8; z = z_hi * 8 + z_lo), core: 2. Of those that a mesh axis runs over, the one named last changes fastest.
Arguments:
- points: float32 [8192, 256], P('pts'), may hold values from -6 to 6
- labels: bfloat16 [8192, 256], P('pts'), may hold values from -6 to 6
- centres: float32 [2, 4096, 256], P(None, 'ctr'), may hold values from -6 to 6
- coeffs: float32 [2, 4096, 256], P(None, 'pts'), may hold values from -6 to 6
- diag_inverse: float32 [2, 4096, 4096], P(None, 'ctr', 'pts'), may hold values from -0.09375 to 0.09375
- off_block: float32 [4096, 4096], P('pts', 'ctr'), may hold values from -0.09375 to 0.09375
Outputs:
- transposed: float32 [2, 4096, 256], P(None, 'ctr', 'pts')
All inputs are finite; a program needn't handle non-finite values.
Results may differ from a plain program's by a relative error of at most 0.0003.
Values sent between devices are 32-bit elements; how exact they have to be, the bound alone decides.
No kernel may reach another device: no remote copies, remote signals or barrier semaphores. Data moves between devices by JAX's collectives and lax.ppermute only.
A program may use at most 64 MiB of HBM per device.

v0:
```python
import math
import jax
import jax.numpy as jnp
from jax import lax
from jax.sharding import PartitionSpec as P


def kernel_tile(points, flat_centres):
    score = lax.dot_general(
        points,
        flat_centres,
        (((1,), (1,)), ((), ())),
        precision=lax.Precision.HIGHEST,
        preferred_element_type=jnp.float32,
    ) / math.sqrt(points.shape[1])
    return score + score * score * score / 3.0


def local(points, labels, centres, coeffs, diag_inverse, off_block):
    high = lax.Precision.HIGHEST
    panels = centres.shape[0]
    local_rows = centres.shape[1]
    flat_centres = centres.reshape(panels * local_rows, centres.shape[2])
    kernel = kernel_tile(points, flat_centres)
    second = lax.psum(
        jnp.dot(diag_inverse[1], coeffs[1], precision=high, preferred_element_type=jnp.float32),
        "pts",
    )
    carried = lax.psum(
        jnp.dot(off_block, second, precision=high, preferred_element_type=jnp.float32), "ctr"
    )
    rest = coeffs[0] - carried
    first = lax.psum(
        jnp.dot(diag_inverse[0], rest, precision=high, preferred_element_type=jnp.float32), "pts"
    )
    solved = jnp.concatenate([first, second], axis=0)
    total_centres = panels * local_rows * lax.axis_size("ctr")
    pred_scale = 1.0 / (2.0 * math.sqrt(total_centres))
    partial_pred = jnp.dot(kernel, solved, precision=high, preferred_element_type=jnp.float32)
    pred = lax.psum(partial_pred, "ctr")
    weights = jnp.tanh(pred * pred_scale - labels.astype(jnp.float32))
    total_points = points.shape[0] * lax.axis_size("pts")
    term = lax.dot_general(
        kernel,
        weights,
        (((0,), (0,)), ((), ())),
        precision=high,
        preferred_element_type=jnp.float32,
    )
    term = term.reshape(panels, local_rows, weights.shape[1])
    summed = lax.psum_scatter(term, "pts", scatter_dimension=2, tiled=True)
    return summed / (2.0 * math.sqrt(total_points))


def solution(mesh):
    return jax.shard_map(
        local,
        mesh=mesh,
        in_specs=(
            P("pts", None),
            P("pts", None),
            P(None, "ctr", None),
            P(None, "pts", None),
            P(None, "ctr", "pts"),
            P("pts", "ctr"),
        ),
        out_specs=P(None, "ctr", "pts"),
        check_vma=False,
    )
```

profile of v0, /device:TPU:8, one launch (start us, length us, event | category | flops | bytes accessed | tf_op | source)
XLA Modules:
  0.0 1540.9 jit_solution(7603430247279964926)
XLA Ops:
  6.5 0.0 copy-start
  6.5 2.0 fusion.11
  8.6 0.0 all-reduce.5.cloned.1.call-update
  8.6 0.0 all-reduce.7.cloned.1.call-start
  8.6 259.4 %all-reduce.5.cloned.1.call-done = f32[128,256]{1,0:T(8,128)} async-done(((f32[128,256]{1,0:T(8,128)}), f32[128,256]{1,0:T(8,128)}) %all-reduce.5.cloned.1.call-update) | async-done | bytes 131088 | tf_op jit(solution)/shard_map/psum | solution.py:25
  268.0 2.0 convolution_bitcast_fusion
  270.0 0.0 all-reduce.7.cloned.1.call-update
  270.0 0.0 all-reduce.9.cloned.1.call-start
  270.1 452.3 %all-reduce.7.cloned.1.call-done = f32[256,256]{1,0:T(8,128)} async-done(((f32[256,256]{1,0:T(8,128)}), f32[256,256]{1,0:T(8,128)}) %all-reduce.7.cloned.1.call-update) | async-done | bytes 262160 | tf_op jit(solution)/shard_map/psum | solution.py:29
  722.4 0.0 copy-done.4
  722.4 2.0 convolution_bitcast_fusion.1
  724.4 0.0 all-reduce.9.cloned.1.call-update
  724.4 0.0 all-reduce.11.cloned.1.call-start
  724.5 0.6 fusion.1
  725.1 251.9 %all-reduce.9.cloned.1.call-done = f32[128,256]{1,0:T(8,128)} async-done(((f32[128,256]{1,0:T(8,128)}), f32[128,256]{1,0:T(8,128)}) %all-reduce.9.cloned.1.call-update) | async-done | bytes 131088 | tf_op jit(solution)/shard_map/psum | solution.py:33
  977.1 2.3 fusion.7
  979.4 0.0 all-reduce.11.cloned.1.call-update
  979.4 0.0 reduce-scatter.2.cloned.1.call-start
  979.4 453.7 %all-reduce.11.cloned.1.call-done = f32[512,256]{1,0:T(8,128)} async-done(((f32[512,256]{1,0:T(8,128)}), f32[512,256]{1,0:T(8,128)}) %all-reduce.11.cloned.1.call-update) | async-done | bytes 524304 | tf_op jit(solution)/shard_map/psum | solution.py:40
  1433.2 2.0 fusion.2
  1435.2 0.8 copy.7
  1436.0 0.0 reduce-scatter.2.cloned.1.call-update
  1436.1 96.9 %reduce-scatter.2.cloned.1.call-done = f32[2,128,16]{1,2,0:T(8,128)} async-done(((f32[2,128,256]{1,2,0:T(8,128)}), f32[2,128,16]{1,2,0:T(8,128)}) %reduce-scatter.2.cloned.1.call-update) | async-done | bytes 16400 | tf_op jit(solution)/shard_map/reduce_scatter | solution.py:51
  1533.0 1.3 broadcast_multiply_fusion
  (13 shorter events, 0.0 us)
Async XLA Ops:
  6.5 717.9 %copy-start = (f32[512,256]{1,0:T(8,128)S(1)}, f32[512,256]{1,0:T(8,128)}, u32[]{:S(2)}) copy-start(f32[512,256]{1,0:T(8,128)} %param.6) | copy-start | bytes 1572868
  6.5 261.5 %all-reduce.5.cloned.1.call-start = ((), (), s32[]{:S(2)}) async-start(), calls=%async_computation.1 | async-start | bytes 262144 | tf_op jit(solution)/shard_map/psum | solution.py:25
  6.5 261.5 %copy-start.6 = (f32[256,128]{1,0:T(8,128)S(1)}, f32[256,128]{1,0:T(8,128)}, u32[]{:S(2)}) copy-start(f32[256,128]{1,0:T(8,128)} %param.11) | copy-start | bytes 393220
  8.6 713.9 %copy-start.1 = (f32[2,256,256]{2,1,0:T(8,128)S(1)}, f32[2,256,256]{2,1,0:T(8,128)}, u32[]{:S(2)}) copy-start(f32[2,256,256]{2,1,0:T(8,128)} %param.9) | copy-start | bytes 1572868
  8.6 713.8 %all-reduce.7.cloned.1.call-start = ((), (), s32[]{:S(2)}) async-start(), calls=%async_computation.2 | async-start | bytes 524288 | tf_op jit(solution)/shard_map/psum | solution.py:29
  270.0 452.4 %copy-start.4 = (f32[2,128,256]{2,1,0:T(8,128)S(1)}, f32[2,128,256]{2,1,0:T(8,128)}, u32[]{:S(2)}) copy-start(f32[2,128,256]{2,1,0:T(8,128)} %param.10) | copy-start | bytes 786436
  270.0 707.0 %all-reduce.9.cloned.1.call-start = ((), (), s32[]{:S(2)}) async-start(), calls=%async_computation.3 | async-start | bytes 262144 | tf_op jit(solution)/shard_map/psum | solution.py:33
  722.4 2.0 copy-start.3
  724.4 708.7 %all-reduce.11.cloned.1.call-start = ((), (), s32[]{:S(2)}) async-start(), calls=%async_computation.4 | async-start | bytes 1048576 | tf_op jit(solution)/shard_map/psum | solution.py:40
  724.5 252.6 %copy-start.2 = (f32[128,256]{1,0:T(8,128)S(1)}, f32[128,256]{1,0:T(8,128)}, u32[]{:S(2)}) copy-start(f32[128,256]{1,0:T(8,128)} %all-reduce.5.cloned.1.call-done) | copy-start | bytes 393220
  979.4 453.8 %copy-start.5 = (bf16[512,256]{1,0:T(8,128)(2,1)S(1)}, bf16[512,256]{1,0:T(8,128)(2,1)}, u32[]{:S(2)}) copy-start(bf16[512,256]{1,0:T(8,128)(2,1)} %param.7) | copy-start | bytes 786436
  979.4 553.6 %reduce-scatter.2.cloned.1.call-start = ((), (), s32[]{:S(2)}) async-start(), calls=%async_computation.5 | async-start | bytes 278528 | tf_op jit(solution)/shard_map/reduce_scatter | solution.py:51
Sparse Core Ops, SparseCore 0:
  10.3 257.7 all-reduce.4
  271.2 451.2 all-reduce.6
  725.3 251.7 all-reduce.8
  980.1 453.0 all-reduce.10
  1437.6 95.3 reduce-scatter.1
where the time goes:
time: 1540 us
  waiting for transfers between devices  1510 us (98%)
    psum x1, waiting for transfers between devices, local(): pred = lax.psum(partial_pred, 'ctr')  454 us
    psum x1, waiting for transfers between devices, local(): lax.psum(jnp.dot(off_block, second, precision=high, preferred_element_typ...  452 us
    psum x1, waiting for transfers between devices, local(): lax.psum(jnp.dot(diag_inverse[1], coeffs[1], precision=high, preferred_el...  259 us
    psum x1, waiting for transfers between devices, local(): lax.psum(jnp.dot(diag_inverse[0], rest, precision=high, preferred_element...  252 us
    reduce_scatter x1, waiting for transfers between devices, local(): summed = lax.psum_scatter(term, 'pts', scatter_dimension=2, tiled=True)  96.9 us
  transfers between devices with their start and end apart: 5, of which 5 were waited for; matrix products, arithmetic and copies ran while one was open for 0% of the time, Pallas kernels for 0%

commit v1 on v0

--- a/solution.py
+++ b/solution.py
@@ -37,7 +37,7 @@
     total_centres = panels * local_rows * lax.axis_size("ctr")
     pred_scale = 1.0 / (2.0 * math.sqrt(total_centres))
     partial_pred = jnp.dot(kernel, solved, precision=high, preferred_element_type=jnp.float32)
-    pred = lax.psum(partial_pred, "ctr")
+    pred = jnp.sum(lax.all_gather(partial_pred, "ctr"), axis=0)
     weights = jnp.tanh(pred * pred_scale - labels.astype(jnp.float32))
     total_points = points.shape[0] * lax.axis_size("pts")
     term = lax.dot_general(

time: 1540 us -> 1340 us (0.87)
  waiting for transfers between devices: 1510 us -> 1310 us
    psum x1 -> x0, waiting for transfers between devices: 454 us -> none  [local(): pred = lax.psum(partial_pred, 'ctr')]
    all_gather x0 -> x1, waiting for transfers between devices: none -> 254 us  [local(): pred = jnp.sum(lax.all_gather(partial_pred, 'ctr'), axis=0)]
where the time goes in v1:
time: 1340 us
  waiting for transfers between devices  1310 us (98%)
    psum x1, waiting for transfers between devices, local(): lax.psum(jnp.dot(off_block, second, precision=high, preferred_element_typ...  452 us
    psum x1, waiting for transfers between devices, local(): lax.psum(jnp.dot(diag_inverse[1], coeffs[1], precision=high, preferred_el...  259 us
    all_gather x1, waiting for transfers between devices, local(): pred = jnp.sum(lax.all_gather(partial_pred, 'ctr'), axis=0)  254 us
    psum x1, waiting for transfers between devices, local(): lax.psum(jnp.dot(diag_inverse[0], rest, precision=high, preferred_element...  251 us
    reduce_scatter x1, waiting for transfers between devices, local(): summed = lax.psum_scatter(term, 'pts', scatter_dimension=2, tiled=True)  94.3 us
  transfers between devices with their start and end apart: 5, of which 5 were waited for; matrix products, arithmetic and copies ran while one was open for 0% of the time, Pallas kernels for 0%

profile of v1, /device:TPU:8, one launch (start us, length us, event | category | flops | bytes accessed | tf_op | source)
XLA Modules:
  0.0 1344.6 jit_solution(15388619705694062944)
XLA Ops:
  6.5 0.0 copy-start
  6.5 2.0 fusion.11
  8.6 0.0 all-reduce.4.cloned.1.call-update
  8.6 0.0 all-reduce.6.cloned.1.call-start
  8.6 259.4 %all-reduce.4.cloned.1.call-done = f32[128,256]{1,0:T(8,128)} async-done(((f32[128,256]{1,0:T(8,128)}), f32[128,256]{1,0:T(8,128)}) %all-reduce.4.cloned.1.call-update) | async-done | bytes 131088 | tf_op jit(solution)/shard_map/psum | solution.py:25
  268.0 2.0 convolution_bitcast_fusion
  270.1 0.0 all-reduce.6.cloned.1.call-update
  270.1 0.0 all-reduce.8.cloned.1.call-start
  270.1 452.3 %all-reduce.6.cloned.1.call-done = f32[256,256]{1,0:T(8,128)} async-done(((f32[256,256]{1,0:T(8,128)}), f32[256,256]{1,0:T(8,128)}) %all-reduce.6.cloned.1.call-update) | async-done | bytes 262160 | tf_op jit(solution)/shard_map/psum | solution.py:29
  722.4 2.0 convolution_bitcast_fusion.1
  724.5 0.0 all-reduce.8.cloned.1.call-update
  724.5 0.0 all-gather.3.cloned.1.call-start
  724.6 1.6 fusion.1
  726.2 250.9 %all-reduce.8.cloned.1.call-done = f32[128,256]{1,0:T(8,128)} async-done(((f32[128,256]{1,0:T(8,128)}), f32[128,256]{1,0:T(8,128)}) %all-reduce.8.cloned.1.call-update) | async-done | bytes 131088 | tf_op jit(solution)/shard_map/psum | solution.py:33
  977.1 2.3 fusion.7
  979.4 0.0 all-gather.3.cloned.1.call-update
  979.4 0.0 reduce-scatter.2.cloned.1.call-start
  979.5 254.3 %all-gather.3.cloned.1.call-done = f32[16384,256]{1,0:T(8,128)} async-done(((f32[512,256]{1,0:T(8,128)}), f32[16384,256]{1,0:T(8,128)}) %all-gather.3.cloned.1.call-update) | async-done | bytes 16777232 | tf_op jit(solution)/shard_map/all_gather | solution.py:40
  1233.7 6.9 reduce_sum.9
  1240.7 1.0 fusion.2
  1241.7 0.8 copy.7
  1242.5 0.0 reduce-scatter.2.cloned.1.call-update
  1242.5 94.3 %reduce-scatter.2.cloned.1.call-done = f32[2,128,16]{1,2,0:T(8,128)} async-done(((f32[2,128,256]{1,2,0:T(8,128)}), f32[2,128,16]{1,2,0:T(8,128)}) %reduce-scatter.2.cloned.1.call-update) | async-done | bytes 16400 | tf_op jit(solution)/shard_map/reduce_scatter | solution.py:51
  1336.8 1.3 broadcast_multiply_fusion
  (4 shorter events, 0.0 us)
Async XLA Ops:
  6.5 718.0 %copy-start = (f32[512,256]{1,0:T(8,128)S(1)}, f32[512,256]{1,0:T(8,128)}, u32[]{:S(2)}) copy-start(f32[512,256]{1,0:T(8,128)} %param.6) | copy-start | bytes 1572868
  6.5 1234.1 %copy-start.1 = (bf16[512,256]{1,0:T(8,128)(2,1)S(1)}, bf16[512,256]{1,0:T(8,128)(2,1)}, u32[]{:S(2)}) copy-start(bf16[512,256]{1,0:T(8,128)(2,1)} %param.7) | copy-start | bytes 786436
  6.5 261.5 %all-reduce.4.cloned.1.call-start = ((), (), s32[]{:S(2)}) async-start(), calls=%async_computation.1 | async-start | bytes 262144 | tf_op jit(solution)/shard_map/psum | solution.py:25
  8.6 713.8 %all-reduce.6.cloned.1.call-start = ((), (), s32[]{:S(2)}) async-start(), calls=%async_computation.2 | async-start | bytes 524288 | tf_op jit(solution)/shard_map/psum | solution.py:29
  270.1 707.0 %all-reduce.8.cloned.1.call-start = ((), (), s32[]{:S(2)}) async-start(), calls=%async_computation.3 | async-start | bytes 262144 | tf_op jit(solution)/shard_map/psum | solution.py:33
  724.5 509.3 %all-gather.3.cloned.1.call-start = ((), (), s32[]{:S(2)}) async-start(), calls=%async_computation.5 | async-start | bytes 17301504 | tf_op jit(solution)/shard_map/all_gather | solution.py:40
  979.4 357.3 %reduce-scatter.2.cloned.1.call-start = ((), (), s32[]{:S(2)}) async-start(), calls=%async_computation.4 | async-start | bytes 278528 | tf_op jit(solution)/shard_map/reduce_scatter | solution.py:51
Sparse Core Ops, SparseCore 0:
  10.3 257.7 all-reduce.3
  271.2 451.2 all-reduce.5
  725.3 251.7 all-reduce.7
  979.6 254.1 all-gather.2
  1242.6 94.1 reduce-scatter.1
